TPU v7x, 32 devices: a whole 2x2x4 slice. The times are simulated.
32 devices in a mesh: groups: 2 (over y), sess: 4 (over z), inner: 2 (over x), rep: 2 (over core).
Axes of the slice: x: 2, y: 2, z: 4, core: 2. Of those that a mesh axis runs over, the one named last changes fastest.
Arguments:
- thinker_rows: bfloat16 [4096, 3584], P(('groups', 'sess', 'rep'), 'inner'), parts along dimension 0, may hold values from -6 to 6
- row_session: int32 [4096, 1], P(('groups', 'sess', 'rep')), parts along dimension 0, may hold values from 0 to 31; in each aligned block of 256 rows (0 to 255, 256 to 511, ...) at most 12 rows name the same one
- speaker_of: int32 [64], P('groups'), parts along dimension 0, may hold values from 0 to 7
- prompt_slot: int32 [16], P('groups'), parts along dimension 0, may hold values from 0 to 7, each once
- prompt_cache: bfloat16 [16, 1024, 1024], P(('groups', 'sess'), ('inner', 'rep')), parts along dimension 0, may hold values from -64 to 64
- proj_weight: bfloat16 [3584, 896], P('inner'), may hold values from -0.09375 to 0.09375
- attn_gain: bfloat16 [896], replicated, may hold values from 0.5 to 1.5
- q_weight: bfloat16 [896, 1536], replicated, may hold values from -0.1875 to 0.1875
- k_weight: bfloat16 [896, 512], replicated, may hold values from -0.625 to 0.625
- v_weight: bfloat16 [896, 512], replicated, may hold values from -0.1875 to 0.1875
- o_weight: bfloat16 [1536, 896], replicated, may hold values from -0.15625 to 0.15625
Outputs:
- voice_states: bfloat16 [64, 96, 896], P(('groups', 'sess', 'inner', 'rep')), parts along dimension 0
There are 2 independent parts, one for each index of `groups`. A program takes and returns all parts, laid end to end along the dimension named above; an argument that names none is the same for every part. Nothing has to cross between parts.
Inputs may be any that keep to these rules, and one draw needn't show every extreme that they name: `row_session`: column 0 names the session of the row. Within each block of 256 rows (rows b * 256 to (b + 1) * 256 - 1, the rows of one index of sess+rep) no session is named by more than 12 rows, a bound that some block reaches; every session is named by some row. `prompt_slot`: each slot holds exactly one speaker's prompt.
All inputs are finite; a program needn't handle non-finite values.
Results may differ from a plain program's by a relative error of at most 0.0071.
Values may be sent and summed in bfloat16 or wider, within the bound.
No kernel may reach another device: no remote copies, remote signals or barrier semaphores. Data moves between devices by JAX's collectives and lax.ppermute only.
A program may use at most 128 MiB of HBM per device.

v0:
```python
import jax
import jax.numpy as jnp
from jax import lax
from jax.sharding import PartitionSpec as P

H = 12
KVH = 4
HD = 128
PROMPT = 1024
SLOTS = 96
EPSILON = 1e-06
ROPE_BASE = 1000000.0


def rms_scale(states, gain):
    widened = states.astype(jnp.float32)
    factor = lax.rsqrt(jnp.mean(widened * widened, axis=-1, keepdims=True) + EPSILON)
    return (widened * factor * gain.astype(jnp.float32)).astype(jnp.bfloat16)


def rope_tables(slot_total):
    half_width = HD // 2
    inverse = ROPE_BASE ** (-(jnp.arange(half_width, dtype=jnp.float32) * 2.0) / HD)
    angles = (PROMPT + jnp.arange(slot_total)).astype(jnp.float32)[:, None] * inverse[None, :]
    cosine = jnp.concatenate([jnp.cos(angles), jnp.cos(angles)], axis=1)[:, None, :]
    sine_table = jnp.concatenate([jnp.sin(angles), jnp.sin(angles)], axis=1)[:, None, :]
    return (cosine, sine_table)


def rotate(vectors, cosine, sine_table):
    half_width = vectors.shape[-1] // 2
    turned = jnp.concatenate([-vectors[..., half_width:], vectors[..., :half_width]], axis=-1)
    return vectors * cosine + turned * sine_table


def attend(states, lengths, prompts, attn_gain, q_weight, k_weight, v_weight, o_weight):
    session_total, slot_total, model_width = states.shape
    flat_rows = states.reshape(session_total * slot_total, model_width)
    normed = rms_scale(flat_rows, attn_gain)
    cosine, sine_table = rope_tables(slot_total)
    query = rotate(
        jnp.dot(normed, q_weight, preferred_element_type=jnp.float32).reshape(
            session_total, slot_total, H, HD
        ),
        cosine,
        sine_table,
    ).astype(jnp.bfloat16)
    own_keys = rotate(
        jnp.dot(normed, k_weight, preferred_element_type=jnp.float32).reshape(
            session_total, slot_total, KVH, HD
        ),
        cosine,
        sine_table,
    ).astype(jnp.bfloat16)
    own_values = (
        jnp.dot(normed, v_weight, preferred_element_type=jnp.float32)
        .reshape(session_total, slot_total, KVH, HD)
        .astype(jnp.bfloat16)
    )
    prompt_keys = prompts[:, :, : KVH * HD].reshape(session_total, PROMPT, KVH, HD)
    prompt_values = prompts[:, :, KVH * HD :].reshape(session_total, PROMPT, KVH, HD)
    all_keys = jnp.concatenate([prompt_keys, own_keys], axis=1)
    all_values = jnp.concatenate([prompt_values, own_values], axis=1)
    key_place = jnp.arange(PROMPT + slot_total) - PROMPT
    query_place = jnp.arange(slot_total)
    allowed = (key_place[None, None, :] < 0) | (
        key_place[None, None, :] <= query_place[None, :, None]
    ) & (key_place[None, None, :] < lengths[:, None, None])
    per_group = H // KVH
    outputs = []
    for kv_head in range(KVH):
        query_group = query[:, :, kv_head * per_group : (kv_head + 1) * per_group]
        scores = jnp.einsum(
            "cqhd,ckd->chqk",
            query_group,
            all_keys[:, :, kv_head],
            preferred_element_type=jnp.float32,
        ) * HD ** (-0.5)
        scores = jnp.where(allowed[:, None], scores, -1e30)
        highest = jnp.max(scores, axis=-1, keepdims=True)
        powers = jnp.exp(scores - highest)
        weights = (powers / jnp.sum(powers, axis=-1, keepdims=True)).astype(jnp.bfloat16)
        outputs.append(
            jnp.einsum(
                "chqk,ckd->cqhd",
                weights,
                all_values[:, :, kv_head],
                preferred_element_type=jnp.float32,
            )
        )
    attended = (
        jnp.concatenate(outputs, axis=2)
        .reshape(session_total * slot_total, H * HD)
        .astype(jnp.bfloat16)
    )
    return flat_rows.astype(jnp.float32) + jnp.dot(
        attended, o_weight, preferred_element_type=jnp.float32
    )


def body(
    thinker_rows,
    row_session,
    speaker_of,
    prompt_slot,
    prompt_cache,
    proj_weight,
    attn_gain,
    q_weight,
    k_weight,
    v_weight,
    o_weight,
):
    sess_count = lax.axis_size("sess")
    inner_count = lax.axis_size("inner")
    rep_count = lax.axis_size("rep")
    owner_count = sess_count * rep_count
    session_all = speaker_of.shape[0]
    per_device = session_all // (owner_count * inner_count)
    per_owner = per_device * inner_count
    slot_cap = SLOTS // owner_count
    inner_place = lax.axis_index("inner")
    shard_place = lax.axis_index("sess")
    row_owner = row_session[:, 0]
    device_of = row_owner // per_device
    target = (
        (device_of // (inner_count * rep_count) * rep_count + device_of % rep_count) * per_owner
        + device_of // rep_count % inner_count * per_device
        + row_owner % per_device
    )
    row_order = jnp.arange(row_owner.shape[0])
    earlier = jnp.sum(
        (
            (row_owner[:, None] == row_owner[None, :]) & (row_order[None, :] < row_order[:, None])
        ).astype(jnp.int32),
        axis=1,
    )
    slot_place = target * slot_cap + earlier
    counts = jnp.sum(
        (target[:, None] == jnp.arange(owner_count * per_owner)[None, :]).astype(jnp.int32), axis=0
    ).reshape(owner_count, per_owner)
    partial_sum = jnp.dot(thinker_rows, proj_weight, preferred_element_type=jnp.float32)
    own_columns = lax.psum_scatter(partial_sum, "inner", scatter_dimension=1, tiled=True).astype(
        jnp.bfloat16
    )
    buffer = (
        jnp.zeros((owner_count * per_owner * slot_cap, own_columns.shape[1]), own_columns.dtype)
        .at[slot_place]
        .set(own_columns)
    )
    arrived = lax.all_to_all(
        buffer.reshape(owner_count, per_owner * slot_cap, own_columns.shape[1]),
        ("sess", "rep"),
        split_axis=0,
        concat_axis=0,
        tiled=True,
    )
    counts_in = lax.all_to_all(counts, ("sess", "rep"), split_axis=0, concat_axis=0, tiled=True)
    arrived_rows = arrived.reshape(owner_count, per_owner, slot_cap, arrived.shape[2])
    regrouped = lax.all_to_all(arrived_rows, "inner", split_axis=1, concat_axis=3, tiled=True)
    projected = jnp.transpose(regrouped, (1, 0, 2, 3)).reshape(
        per_device, owner_count * slot_cap, regrouped.shape[3]
    )
    own_counts = lax.dynamic_slice_in_dim(counts_in, inner_place * per_device, per_device, 1)
    offsets = jnp.cumsum(own_counts, axis=0) - own_counts
    lengths = jnp.sum(own_counts, axis=0)
    within = jnp.arange(slot_cap)
    position = jnp.transpose(offsets)[:, :, None] + within[None, None, :]
    live_slot = within[None, None, :] < jnp.transpose(own_counts)[:, :, None]
    position = jnp.where(live_slot, position, SLOTS).reshape(per_device, owner_count * slot_cap)
    session_rows = jnp.broadcast_to(jnp.arange(per_device)[:, None], position.shape)
    compact = (
        jnp.zeros((per_device, SLOTS, projected.shape[2]), jnp.bfloat16)
        .at[session_rows, position]
        .set(projected, mode="drop")
    )
    shard_sessions = per_device * inner_count * rep_count
    wanted_speaker = lax.dynamic_slice_in_dim(
        speaker_of, shard_place * shard_sessions, shard_sessions
    )
    speaker_table = jnp.arange(prompt_slot.shape[0])
    wanted_slot = jnp.sum(
        jnp.where(wanted_speaker[:, None] == speaker_table[None, :], prompt_slot[None, :], 0),
        axis=1,
    )
    piece = lax.all_gather(prompt_cache, "sess", axis=0, tiled=True)
    matching = (wanted_slot[:, None] == jnp.arange(piece.shape[0])[None, :]).astype(jnp.bfloat16)
    chosen = jnp.einsum("sp,ptc->stc", matching, piece, preferred_element_type=jnp.float32)
    prompts = lax.all_to_all(
        chosen.astype(jnp.bfloat16), ("inner", "rep"), split_axis=0, concat_axis=1, tiled=True
    )
    summed = attend(compact, lengths, prompts, attn_gain, q_weight, k_weight, v_weight, o_weight)
    live_rows = (jnp.arange(SLOTS)[None, :] < lengths[:, None]).reshape(-1, 1)
    return (
        jnp.where(live_rows, summed, 0.0)
        .astype(jnp.bfloat16)
        .reshape(per_device, SLOTS, summed.shape[1])
    )


def solution(mesh):
    in_specs = (
        P(("groups", "sess", "rep"), "inner"),
        P(("groups", "sess", "rep"), None),
        P("groups"),
        P("groups"),
        P(("groups", "sess"), ("inner", "rep"), None),
        P("inner", None),
        P(),
        P(),
        P(),
        P(),
        P(),
    )
    out_specs = P(("groups", "sess", "inner", "rep"), None, None)
    return jax.shard_map(body, mesh=mesh, in_specs=in_specs, out_specs=out_specs, check_vma=False)
```

profile of v0, /device:TPU:0, one launch (start us, length us, event | category | flops | bytes accessed | tf_op | source)
XLA Modules:
  0.0 214.4 jit_solution(5181493876565836849)
XLA Ops:
  9.3 3.5 %fusion.175 = f32[256,896]{0,1:T(8,128)} fusion(bf16[256,1792]{1,0:T(8,128)(2,1)} %param.11, bf16[1792,896]{1,0:T(8,128)(2,1)S(1)} %copy-done), kind=kOutput, calls=%fused_computation.189 | convolution fusion | flops 822083584 | bytes 5046272 | tf_op jit(solution)/shard_map/dot_general | solution.py:142
  14.4 6.3 %all-to-all-start = ((s32[8,1,4]{2,1,0:T(1,128)}), s32[8,1,4]{2,1,0:T(1,128)S(1)}, u32[]{:S(2)}, u32[]{:S(2)}) async-start(s32[8,1,4]{2,1,0:T(1,128)} %bitcast.1), calls=%async_computation | async-start | bytes 8192 | tf_op jit(solution)/shard_map/all_to_all | solution.py:158
  20.7 4.9 %copy.90 = bf16[896,1536]{0,1:T(8,128)(2,1)} copy(bf16[896,1536]{1,0:T(8,128)(2,1)} %param.18) | data formatting | bytes 5505024 | tf_op args[7]
  29.3 5.2 %reduce-scatter.2.cloned.1.call-done = f32[256,448]{0,1:T(8,128)} async-done(((f32[256,896]{0,1:T(8,128)}), f32[256,448]{0,1:T(8,128)}) %reduce-scatter.2.cloned.1.call-update) | async-done | bytes 458768 | tf_op jit(solution)/shard_map/reduce_scatter | solution.py:143
  38.0 4.6 %all-to-all-start.1 = ((bf16[8,48,448]{2,1,0:T(8,128)(2,1)}), bf16[8,48,448]{2,1,0:T(8,128)(2,1)S(1)}, u32[]{:S(2)}, u32[]{:S(2)}) async-start(bf16[8,48,448]{2,1,0:T(8,128)(2,1)} %bitcast.8), calls=%async_computation.2 | async-start | bytes 786432 | tf_op jit(solution)/shard_map/all_to_all | solution.py:151
  43.7 24.4 %all-to-all-done.1 = bf16[8,48,448]{2,1,0:T(8,128)(2,1)S(1)} async-done(((bf16[8,48,448]{2,1,0:T(8,128)(2,1)}), bf16[8,48,448]{2,1,0:T(8,128)(2,1)S(1)}, u32[]{:S(2)}, u32[]{:S(2)}) %all-to-all-start.1) | async-done | bytes 344096 | tf_op jit(solution)/shard_map/all_to_all | solution.py:151
  69.1 3.5 %all-to-all-start.2 = ((bf16[8,4,12,448]{3,0,2,1:T(8,128)(2,1)}), bf16[8,4,12,448]{3,0,2,1:T(8,128)(2,1)S(1)}, u32[]{:S(2)}, u32[]{:S(2)}) async-start(bf16[8,4,12,448]{3,0,2,1:T(8,128)(2,1)} %bitcast.9), calls=%async_computation.3 | async-start | bytes 786432 | tf_op jit(solution)/shard_map/all_to_all | solution.py:160
  72.5 33.9 %all-gather.2.cloned.1.call-done = bf16[8,256,1024]{2,1,0:T(8,128)(2,1)} async-done(((bf16[2,256,1024]{2,1,0:T(8,128)(2,1)}), bf16[8,256,1024]{2,1,0:T(8,128)(2,1)}) %all-gather.2.cloned.1.call-update) | async-done | bytes 4194320 | tf_op jit(solution)/shard_map/all_gather | solution.py:186
  106.4 4.7 %fusion.22 = bf16[8,256,1024]{2,0,1:T(8,128)(2,1)S(1)} fusion(bf16[8,256,1024]{2,1,0:T(8,128)(2,1)} %all-gather.2.cloned.1.call-done, s32[8]{0:T(128)S(1)} %select_reduce_fusion), kind=kOutput, calls=%fused_computation.34 | convolution fusion | flops 35651648 | bytes 8388640 | tf_op jit(solution)/shard_map/sp,ptc->stc/dot_general | solution.py:188
  111.2 4.3 %copy.80 = bf16[8,256,1024]{2,1,0:T(8,128)(2,1)} copy(bf16[8,256,1024]{2,0,1:T(8,128)(2,1)S(1)} %fusion.22) | data formatting | bytes 8388608 | tf_op jit(solution)/shard_map/convert_element_type | solution.py:190
  115.4 5.0 %all-to-all-start.3 = ((bf16[8,256,1024]{2,1,0:T(8,128)(2,1)}), bf16[8,256,1024]{2,1,0:T(8,128)(2,1)}, u32[]{:S(2)}, u32[]{:S(2)}) async-start(bf16[8,256,1024]{2,1,0:T(8,128)(2,1)} %copy.80), calls=%async_computation.4 | async-start | bytes 8388608 | tf_op jit(solution)/shard_map/all_to_all | solution.py:189
  122.3 13.1 %scatter_fusion = bf16[2,96,896]{2,1,0:T(8,128)(2,1)S(1)} fusion(bf16[2,96,896]{2,1,0:T(8,128)(2,1)S(1)} %broadcast_in_dim.55, s32[192]{0:T(256)S(1)} %reshape.305, bf16[192,896]{1,0:T(8,128)(2,1)S(1)} %reshape.307), kind=kCustom, calls=%fused_computation.1 | custom fusion | bytes 1033728 | tf_op jit(solution)/shard_map/scatter | solution.py:175
  140.3 28.3 %all-to-all-done.3 = bf16[8,256,1024]{2,1,0:T(8,128)(2,1)} async-done(((bf16[8,256,1024]{2,1,0:T(8,128)(2,1)}), bf16[8,256,1024]{2,1,0:T(8,128)(2,1)}, u32[]{:S(2)}, u32[]{:S(2)}) %all-to-all-start.3) | async-done | bytes 4194336 | tf_op jit(solution)/shard_map/all_to_all | solution.py:189
  168.5 2.6 %copy.81 = bf16[2,4,256,1024]{3,2,1,0:T(8,128)(2,1)S(1)} copy(bf16[2,4,256,1024]{3,2,0,1:T(8,128)(2,1)} %bitcast.16) | data formatting | bytes 8388608 | tf_op jit(solution)/shard_map/all_to_all | solution.py:189
  171.1 2.5 %fusion.154 = (bf16[2,1024,512]{2,1,0:T(8,128)(2,1)}, bf16[2,1024,512]{2,1,0:T(8,128)(2,1)}) fusion(bf16[2,1024,1024]{2,1,0:T(8,128)(2,1)S(1)} %bitcast.185), kind=kLoop, calls=%fused_computation.184 | loop fusion | bytes 8388608 | tf_op jit(solution)/shard_map/slice | solution.py:61
  173.6 3.0 %copy.86 = bf16[2,1024,512]{1,2,0:T(8,128)(2,1)S(1)} copy(bf16[2,1024,512]{2,1,0:T(8,128)(2,1)} %get-tuple-element.10) | data formatting | bytes 4194304 | tf_op jit(solution)/shard_map/slice | solution.py:60
  176.7 2.5 %copy.88 = bf16[2,1024,4,128]{3,1,0,2:T(8,128)(2,1)} copy(bf16[2,1024,4,128]{1,3,2,0:T(8,128)(2,1)S(1)} %bitcast.187) | data formatting | bytes 4194304 | tf_op jit(solution)/shard_map/reshape | solution.py:60
  179.2 3.8 %fusion.155 = (f32[2,3,96]{2,1,0:T(4,128)S(1)}, f32[2,3,96,1120]{3,2,1,0:T(8,128)}) fusion(pred[2,96,1120]{2,1,0:T(8,128)(4,1)S(1)} %copy-done.9, bf16[2,1024,4,128]{3,1,0,2:T(8,128)(2,1)} %copy.88, bf16[2,96,12,128]{3,1,2,0:T(8,128)(2,1)S(1)} %fusion.32, bf16[2,96,4,128]{3,1,2,0:T(8,128)(2,1)S(1)} %copy-done.10), kind=kOutput, calls=%fused_computation.185 | convolution fusion | flops 168879200 | bytes 5245184 | tf_op jit(solution)/shard_map/sub | solution.py:81
  183.0 2.6 %fusion.160 = (f32[2,3,96]{2,1,0:T(4,128)S(1)}, f32[2,3,96,1120]{3,2,1,0:T(8,128)}) fusion(pred[2,96,1120]{2,1,0:T(8,128)(4,1)S(1)} %copy-done.9, bf16[2,1024,4,128]{3,1,0,2:T(8,128)(2,1)S(1)} %copy-done.4, bf16[2,96,12,128]{3,1,2,0:T(8,128)(2,1)S(1)} %fusion.32, bf16[2,96,4,128]{3,1,2,0:T(8,128)(2,1)S(1)} %copy-done.10), kind=kOutput, calls=%fused_computation.186 | convolution fusion | flops 168879200 | bytes 5245184 | tf_op jit(solution)/shard_map/sub | solution.py:81
  185.7 2.6 %fusion.165 = (f32[2,3,96]{2,1,0:T(4,128)S(1)}, f32[2,3,96,1120]{3,2,1,0:T(8,128)}) fusion(pred[2,96,1120]{2,1,0:T(8,128)(4,1)S(1)} %copy-done.9, bf16[2,1024,4,128]{3,1,0,2:T(8,128)(2,1)S(1)} %copy-done.4, bf16[2,96,12,128]{3,1,2,0:T(8,128)(2,1)S(1)} %fusion.32, bf16[2,96,4,128]{3,1,2,0:T(8,128)(2,1)S(1)} %copy-done.10), kind=kOutput, calls=%fused_computation.187 | convolution fusion | flops 168879200 | bytes 5245184 | tf_op jit(solution)/shard_map/sub | solution.py:81
  188.3 2.7 %fusion.170 = (f32[2,3,96]{2,1,0:T(4,128)S(1)}, f32[2,3,96,1120]{3,2,1,0:T(8,128)}) fusion(pred[2,96,1120]{2,1,0:T(8,128)(4,1)S(1)} %copy-done.9, bf16[2,1024,4,128]{3,1,0,2:T(8,128)(2,1)S(1)} %copy-done.4, bf16[2,96,12,128]{3,1,2,0:T(8,128)(2,1)S(1)} %fusion.32, bf16[2,96,4,128]{3,1,2,0:T(8,128)(2,1)S(1)} %copy-done.10), kind=kOutput, calls=%fused_computation.188 | convolution fusion | flops 168879200 | bytes 5245184 | tf_op jit(solution)/shard_map/sub | solution.py:81
  190.9 3.0 %copy.82 = bf16[2,1024,512]{1,2,0:T(8,128)(2,1)S(1)} copy(bf16[2,1024,512]{2,1,0:T(8,128)(2,1)} %get-tuple-element.9) | data formatting | bytes 4194304 | tf_op jit(solution)/shard_map/slice | solution.py:61
  193.9 2.9 %copy.84 = bf16[2,1024,4,128]{3,1,0,2:T(8,128)(2,1)} copy(bf16[2,1024,4,128]{1,3,2,0:T(8,128)(2,1)S(1)} %bitcast.188) | data formatting | bytes 4194304 | tf_op jit(solution)/shard_map/reshape | solution.py:61
  196.8 2.6 %fusion.40 = bf16[2,96,3,128]{3,1,2,0:T(8,128)(2,1)S(1)} fusion(f32[2,3,96,1120]{3,2,1,0:T(8,128)} %get-tuple-element.18, f32[2,3,96]{2,1,0:T(4,128)S(1)} %get-tuple-element.17, bf16[2,1024,4,128]{3,1,0,2:T(8,128)(2,1)} %copy.84, bf16[2,96,4,128]{3,1,2,0:T(8,128)(2,1)S(1)} %copy-done.17), kind=kOutput, calls=%fused_computation.64 | convolution fusion | flops 167661568 | bytes 5024000 | tf_op jit(solution)/shard_map/chqk,ckd->cqhd/dot_general | solution.py:84
  (104 shorter events, 26.7 us)
Async XLA Ops:
  7.4 1.9 copy-start
  7.4 6.0 %copy-start.11 = (s32[256,1]{0,1:T(1,128)S(1)}, s32[256,1]{0,1:T(1,128)}, u32[]{:S(2)}) copy-start(s32[256,1]{0,1:T(1,128)} %param.12) | copy-start | bytes 3076
  7.4 27.1 %reduce-scatter.2.cloned.1.call-start = ((), (), s32[]{:S(2)}) async-start(), calls=%async_computation.5 | async-start | bytes 1376256 | tf_op jit(solution)/shard_map/reduce_scatter | solution.py:143
  12.8 93.7 %all-gather.2.cloned.1.call-start = ((), (), s32[]{:S(2)}) async-start(), calls=%async_computation.6 | async-start | bytes 5242880 | tf_op jit(solution)/shard_map/all_gather | solution.py:186
  14.4 14.6 %all-to-all-start = ((s32[8,1,4]{2,1,0:T(1,128)}), s32[8,1,4]{2,1,0:T(1,128)S(1)}, u32[]{:S(2)}, u32[]{:S(2)}) async-start(s32[8,1,4]{2,1,0:T(1,128)} %bitcast.1), calls=%async_computation | async-start | bytes 8192 | tf_op jit(solution)/shard_map/all_to_all | solution.py:158
  20.7 5.0 %copy-start.12 = (bf16[896]{0:T(1024)(128)(2,1)S(1)}, bf16[896]{0:T(1024)(128)(2,1)}, u32[]{:S(2)}) copy-start(bf16[896]{0:T(1024)(128)(2,1)} %param.17) | copy-start | bytes 5380
  20.7 5.0 %copy-start.5 = (bf16[896,512]{1,0:T(8,128)(2,1)S(1)}, bf16[896,512]{1,0:T(8,128)(2,1)}, u32[]{:S(2)}) copy-start(bf16[896,512]{1,0:T(8,128)(2,1)} %param.19) | copy-start | bytes 2752516
  20.7 5.6 %copy-start.14 = (s32[32]{0:T(128)S(1)}, s32[32]{0:T(128)}, u32[]{:S(2)}) copy-start(s32[32]{0:T(128)} %param.13) | copy-start | bytes 388
  20.7 5.7 %copy-start.15 = (s32[8]{0:T(128)S(1)}, s32[8]{0:T(128)}, u32[]{:S(2)}) copy-start(s32[8]{0:T(128)} %param.14) | copy-start | bytes 100
  25.6 2.1 copy-start.6
  38.0 30.1 %all-to-all-start.1 = ((bf16[8,48,448]{2,1,0:T(8,128)(2,1)}), bf16[8,48,448]{2,1,0:T(8,128)(2,1)S(1)}, u32[]{:S(2)}, u32[]{:S(2)}) async-start(bf16[8,48,448]{2,1,0:T(8,128)(2,1)} %bitcast.8), calls=%async_computation.2 | async-start | bytes 786432 | tf_op jit(solution)/shard_map/all_to_all | solution.py:151
  69.1 46.4 %all-to-all-start.2 = ((bf16[8,4,12,448]{3,0,2,1:T(8,128)(2,1)}), bf16[8,4,12,448]{3,0,2,1:T(8,128)(2,1)S(1)}, u32[]{:S(2)}, u32[]{:S(2)}) async-start(bf16[8,4,12,448]{3,0,2,1:T(8,128)(2,1)} %bitcast.9), calls=%async_computation.3 | async-start | bytes 786432 | tf_op jit(solution)/shard_map/all_to_all | solution.py:160
  115.4 53.1 %all-to-all-start.3 = ((bf16[8,256,1024]{2,1,0:T(8,128)(2,1)}), bf16[8,256,1024]{2,1,0:T(8,128)(2,1)}, u32[]{:S(2)}, u32[]{:S(2)}) async-start(bf16[8,256,1024]{2,1,0:T(8,128)(2,1)} %copy.80), calls=%async_computation.4 | async-start | bytes 8388608 | tf_op jit(solution)/shard_map/all_to_all | solution.py:189
  136.0 2.2 %copy-start.2 = (bf16[896,1536]{0,1:T(8,128)(2,1)S(1)}, bf16[896,1536]{0,1:T(8,128)(2,1)}, u32[]{:S(2)}) copy-start(bf16[896,1536]{0,1:T(8,128)(2,1)} %copy.90) | copy-start | bytes 8257540
  176.6 2.6 %copy-start.9 = (pred[2,96,1120]{2,1,0:T(8,128)(4,1)S(1)}, pred[2,96,1120]{2,1,0:T(8,128)(4,1)}, u32[]{:S(2)}) copy-start(pred[2,96,1120]{2,1,0:T(8,128)(4,1)} %and_or_fusion) | copy-start | bytes 645124
  176.6 2.6 %copy-start.10 = (bf16[2,96,4,128]{3,1,2,0:T(8,128)(2,1)S(1)}, bf16[2,96,4,128]{3,1,2,0:T(8,128)(2,1)}, u32[]{:S(2)}) copy-start(bf16[2,96,4,128]{3,1,2,0:T(8,128)(2,1)} %fusion.68) | copy-start | bytes 589828
  179.2 3.8 %copy-start.4 = (bf16[2,1024,4,128]{3,1,0,2:T(8,128)(2,1)S(1)}, bf16[2,1024,4,128]{3,1,0,2:T(8,128)(2,1)}, u32[]{:S(2)}) copy-start(bf16[2,1024,4,128]{3,1,0,2:T(8,128)(2,1)} %copy.88) | copy-start | bytes 6291460
  193.9 2.9 %copy-start.17 = (bf16[2,96,4,128]{3,1,2,0:T(8,128)(2,1)S(1)}, bf16[2,96,4,128]{3,1,2,0:T(8,128)(2,1)}, u32[]{:S(2)}) copy-start(bf16[2,96,4,128]{3,1,2,0:T(8,128)(2,1)} %convolution_convert_fusion) | copy-start | bytes 589828
  196.8 2.6 %copy-start.3 = (bf16[2,1024,4,128]{3,1,0,2:T(8,128)(2,1)S(1)}, bf16[2,1024,4,128]{3,1,0,2:T(8,128)(2,1)}, u32[]{:S(2)}) copy-start(bf16[2,1024,4,128]{3,1,0,2:T(8,128)(2,1)} %copy.84) | copy-start | bytes 6291460
  196.8 3.3 %copy-start.20 = (f32[2,3,96,1120]{3,2,1,0:T(8,128)S(1)}, f32[2,3,96,1120]{3,2,1,0:T(8,128)}, u32[]{:S(2)}) copy-start(f32[2,3,96,1120]{3,2,1,0:T(8,128)} %get-tuple-element.20) | copy-start | bytes 7741444
  200.1 1.7 copy-start.19
  201.9 1.7 copy-start.18
  203.6 1.8 copy-start.13
  204.6 2.4 %copy-start.1 = (bf16[1792,896]{1,0:T(8,128)(2,1)S(1)}, bf16[1792,896]{1,0:T(8,128)(2,1)}, u32[]{:S(2)}) copy-start(bf16[1792,896]{1,0:T(8,128)(2,1)} %param.16) | copy-start | bytes 9633796
  (3 other events, 3.6 us)
Sparse Core Ops, SparseCore 0:
  12.9 21.5 reduce-scatter.1
Sparse Core Ops, SparseCore 1:
  14.8 91.6 all-gather.1
where the time goes:
time: 215 us; the launch traced here: 214 us
  waiting for transfers between devices  92.3 us (43%)
  local copies, waits for them, and re-layouts  52.8 us (25%)
  matrix products  28.5 us (13%)
  starting transfers between devices  19.5 us (9%)
  between operations  15.2 us (7%)
  other arithmetic  6.03 us (3%)
    all_gather x1, waiting for transfers between devices, body(): piece = lax.all_gather(prompt_cache, 'sess', axis=0, tiled=True)  33.9 us
    all_to_all x1, waiting for transfers between devices, body(): lax.all_to_all(chosen.astype(jnp.bfloat16), ('inner', 'rep'), split_axis=...  28.3 us
    all_to_all x1, waiting for transfers between devices, body(): lax.all_to_all(buffer.reshape(owner_count, per_owner * slot_cap, own_colu...  24.4 us
    scatter x1, local copies, waits for them, and re-layouts, body(): compact = jnp.zeros((per_device, SLOTS, projected.shape[2]), jnp.bfloat16...  13.1 us
    sub x4, matrix products, attend(): powers = jnp.exp(scores - highest)  11.7 us
    unnamed x43, local copies, waits for them, and re-layouts  10.7 us
    all_to_all x1, starting transfers between devices, body(): lax.all_to_all(counts, ('sess', 'rep'), split_axis=0, concat_axis=0, tile...  6.33 us
    slice x2, local copies, waits for them, and re-layouts, attend(): prompts[:, :, KVH * HD:].reshape(session_total, PROMPT, KVH, HD)  5.48 us
  transfers between devices with their start and end apart: 6, of which 4 were waited for; matrix products, arithmetic and copies ran while one was open for 20% of the time, Pallas kernels for 0%

commit v1 on v0

--- a/solution.py
+++ b/solution.py
@@ -186,8 +186,16 @@
     piece = lax.all_gather(prompt_cache, "sess", axis=0, tiled=True)
     matching = (wanted_slot[:, None] == jnp.arange(piece.shape[0])[None, :]).astype(jnp.bfloat16)
     chosen = jnp.einsum("sp,ptc->stc", matching, piece, preferred_element_type=jnp.float32)
-    prompts = lax.all_to_all(
-        chosen.astype(jnp.bfloat16), ("inner", "rep"), split_axis=0, concat_axis=1, tiled=True
+    prompts = jnp.concatenate(
+        lax.all_to_all(
+            jnp.stack(
+                jnp.split(chosen.astype(jnp.bfloat16), lax.axis_size(("inner", "rep")), axis=0)
+            ),
+            ("inner", "rep"),
+            0,
+            0,
+        ),
+        axis=1,
     )
     summed = attend(compact, lengths, prompts, attn_gain, q_weight, k_weight, v_weight, o_weight)
     live_rows = (jnp.arange(SLOTS)[None, :] < lengths[:, None]).reshape(-1, 1)

time: 215 us -> 227 us (1.056)
  other arithmetic: 6.03 us -> 14.8 us
  local copies, waits for them, and re-layouts: 52.8 us -> 57.5 us
  waiting for transfers between devices: 92.3 us -> 89.8 us
    unnamed x43 -> x47, local copies, waits for them, and re-layouts: 10.7 us -> 20.2 us
    another operation x0 -> x1, other arithmetic: none -> 8.77 us  [body(): jnp.stack(jnp.split(chosen.astype(jnp.bfloat16), lax.axis_size(('inner',...]
    convert_element_type x1 -> x0, local copies, waits for them, and re-layouts: 4.25 us -> none  [body(): chosen.astype(jnp.bfloat16)]
    another operation x0 -> x1, local copies, waits for them, and re-layouts: none -> 3.06 us  [body(): jnp.stack(jnp.split(chosen.astype(jnp.bfloat16), lax.axis_size(('inner',...]
    slice x1 -> x0, local copies, waits for them, and re-layouts: 2.98 us -> none  [attend(): prompts[:, :, :KVH * HD].reshape(session_total, PROMPT, KVH, HD)]
    all_to_all x1 -> x0, local copies, waits for them, and re-layouts: 2.63 us -> none  [body(): lax.all_to_all(chosen.astype(jnp.bfloat16), ('inner', 'rep'), split_axis=...]
    slice x2 -> x1, local copies, waits for them, and re-layouts: 5.48 us -> 6.02 us  [attend(): prompts[:, :, KVH * HD:].reshape(session_total, PROMPT, KVH, HD)]
  transfers between devices with their start and end apart: 6 -> 6, of which waited for: 4 -> 4; matrix products, arithmetic and copies ran while one was open for 20% -> 23% of each run, Pallas kernels for 0% -> 0%
where the time goes in v1:
time: 227 us; the launch traced here: 226 us
  waiting for transfers between devices  89.8 us (40%)
  local copies, waits for them, and re-layouts  57.5 us (25%)
  matrix products  28.5 us (13%)
  starting transfers between devices  20.2 us (9%)
  between operations  15.2 us (7%)
  other arithmetic  14.8 us (7%)
    all_gather x1, waiting for transfers between devices, body(): piece = lax.all_gather(prompt_cache, 'sess', axis=0, tiled=True)  33.2 us
    all_to_all x1, waiting for transfers between devices, body(): lax.all_to_all(jnp.stack(jnp.split(chosen.astype(jnp.bfloat16), lax.axis_...  27.2 us
    all_to_all x1, waiting for transfers between devices, body(): lax.all_to_all(buffer.reshape(owner_count, per_owner * slot_cap, own_colu...  24.4 us
    unnamed x47, local copies, waits for them, and re-layouts  20.2 us
    scatter x1, local copies, waits for them, and re-layouts, body(): compact = jnp.zeros((per_device, SLOTS, projected.shape[2]), jnp.bfloat16...  13.1 us
    sub x4, matrix products, attend(): powers = jnp.exp(scores - highest)  11.7 us
    another operation x1, other arithmetic, body(): jnp.stack(jnp.split(chosen.astype(jnp.bfloat16), lax.axis_size(('inner',...  8.77 us
    all_to_all x1, starting transfers between devices, body(): lax.all_to_all(counts, ('sess', 'rep'), split_axis=0, concat_axis=0, tile...  6.33 us
  transfers between devices with their start and end apart: 6, of which 4 were waited for; matrix products, arithmetic and copies ran while one was open for 23% of the time, Pallas kernels for 0%

profile of v1, /device:TPU:0, one launch (start us, length us, event | category | flops | bytes accessed | tf_op | source)
XLA Modules:
  0.0 226.2 jit_solution(6120638393797086942)
XLA Ops:
  9.3 3.5 %fusion.175 = f32[256,896]{0,1:T(8,128)} fusion(bf16[256,1792]{1,0:T(8,128)(2,1)} %param.11, bf16[1792,896]{1,0:T(8,128)(2,1)S(1)} %copy-done), kind=kOutput, calls=%fused_computation.194 | convolution fusion | flops 822083584 | bytes 5046272 | tf_op jit(solution)/shard_map/dot_general | solution.py:142
  14.4 6.3 %all-to-all-start = ((s32[8,1,4]{2,1,0:T(1,128)}), s32[8,1,4]{2,1,0:T(1,128)S(1)}, u32[]{:S(2)}, u32[]{:S(2)}) async-start(s32[8,1,4]{2,1,0:T(1,128)} %bitcast.1), calls=%async_computation | async-start | bytes 8192 | tf_op jit(solution)/shard_map/all_to_all | solution.py:158
  20.7 4.9 %copy.67 = bf16[896,1536]{0,1:T(8,128)(2,1)} copy(bf16[896,1536]{1,0:T(8,128)(2,1)} %param.18) | data formatting | bytes 5505024 | tf_op args[7]
  30.0 4.5 %reduce-scatter.2.cloned.1.call-done = f32[256,448]{0,1:T(8,128)} async-done(((f32[256,896]{0,1:T(8,128)}), f32[256,448]{0,1:T(8,128)}) %reduce-scatter.2.cloned.1.call-update) | async-done | bytes 458768 | tf_op jit(solution)/shard_map/reduce_scatter | solution.py:143
  38.0 4.6 %all-to-all-start.1 = ((bf16[8,48,448]{2,1,0:T(8,128)(2,1)}), bf16[8,48,448]{2,1,0:T(8,128)(2,1)S(1)}, u32[]{:S(2)}, u32[]{:S(2)}) async-start(bf16[8,48,448]{2,1,0:T(8,128)(2,1)} %bitcast.8), calls=%async_computation.2 | async-start | bytes 786432 | tf_op jit(solution)/shard_map/all_to_all | solution.py:151
  43.7 24.4 %all-to-all-done.1 = bf16[8,48,448]{2,1,0:T(8,128)(2,1)S(1)} async-done(((bf16[8,48,448]{2,1,0:T(8,128)(2,1)}), bf16[8,48,448]{2,1,0:T(8,128)(2,1)S(1)}, u32[]{:S(2)}, u32[]{:S(2)}) %all-to-all-start.1) | async-done | bytes 344096 | tf_op jit(solution)/shard_map/all_to_all | solution.py:151
  69.1 4.2 %all-to-all-start.2 = ((bf16[8,4,12,448]{3,0,2,1:T(8,128)(2,1)}), bf16[8,4,12,448]{3,0,2,1:T(8,128)(2,1)}, u32[]{:S(2)}, u32[]{:S(2)}) async-start(bf16[8,4,12,448]{3,0,2,1:T(8,128)(2,1)} %bitcast.9), calls=%async_computation.3 | async-start | bytes 786432 | tf_op jit(solution)/shard_map/all_to_all | solution.py:160
  73.2 33.2 %all-gather.2.cloned.1.call-done = bf16[8,256,1024]{2,1,0:T(8,128)(2,1)} async-done(((bf16[2,256,1024]{2,1,0:T(8,128)(2,1)}), bf16[8,256,1024]{2,1,0:T(8,128)(2,1)}) %all-gather.2.cloned.1.call-update) | async-done | bytes 4194320 | tf_op jit(solution)/shard_map/all_gather | solution.py:186
  106.4 4.7 %fusion.22 = bf16[8,256,1024]{2,0,1:T(8,128)(2,1)S(1)} fusion(bf16[8,256,1024]{2,1,0:T(8,128)(2,1)} %all-gather.2.cloned.1.call-done, s32[8]{0:T(128)S(1)} %select_reduce_fusion), kind=kOutput, calls=%fused_computation.35 | convolution fusion | flops 35651648 | bytes 8388640 | tf_op jit(solution)/shard_map/sp,ptc->stc/dot_general | solution.py:188
  111.2 3.1 %slice_bitcast_fusion.3 = (bf16[1,2,256,1024]{3,1,2,0:T(2,128)(2,1)S(1)}, bf16[1,2,256,1024]{3,1,2,0:T(2,128)(2,1)S(1)}, bf16[1,2,256,1024]{3,1,2,0:T(2,128)(2,1)S(1)}, bf16[1,2,256,1024]{3,1,2,0:T(2,128)(2,1)S(1)}) fusion(bf16[8,256,1024]{2,0,1:T(8,128)(2,1)S(1)} %fusion.22), kind=kLoop, calls=%fused_computation.69 | loop fusion | bytes 8388608 | tf_op jit(solution)/shard_map/stack | solution.py:191
  114.2 8.8 %pad_maximum_fusion = bf16[4,2,256,1024]{3,1,2,0:T(2,128)(2,1)} fusion(bf16[1,2,256,1024]{3,1,2,0:T(2,128)(2,1)S(1)} %get-tuple-element.12, bf16[1,2,256,1024]{3,1,2,0:T(2,128)(2,1)S(1)} %get-tuple-element.13, bf16[1,2,256,1024]{3,1,2,0:T(2,128)(2,1)S(1)} %get-tuple-element.14, bf16[1,2,256,1024]{3,1,2,0:T(2,128)(2,1)S(1)} %get-tuple-element.11), kind=kLoop, calls=%fused_computation.6 | loop fusion | flops 6291456 | bytes 8388608 | tf_op jit(solution)/shard_map/stack | solution.py:191
  123.0 5.0 %all-to-all-start.3 = ((bf16[4,2,256,1024]{3,1,2,0:T(2,128)(2,1)}), bf16[4,2,256,1024]{3,1,2,0:T(2,128)(2,1)}, u32[]{:S(2)}, u32[]{:S(2)}) async-start(bf16[4,2,256,1024]{3,1,2,0:T(2,128)(2,1)} %pad_maximum_fusion), calls=%async_computation.4 | async-start | bytes 8388608 | tf_op jit(solution)/shard_map/all_to_all | solution.py:190
  130.9 13.1 %scatter_fusion = bf16[2,96,896]{2,1,0:T(8,128)(2,1)S(1)} fusion(bf16[2,96,896]{2,1,0:T(8,128)(2,1)S(1)} %broadcast_in_dim.55, s32[192]{0:T(256)S(1)} %reshape.313, bf16[192,896]{1,0:T(8,128)(2,1)S(1)} %reshape.315), kind=kCustom, calls=%fused_computation.1 | custom fusion | bytes 1033728 | tf_op jit(solution)/shard_map/scatter | solution.py:175
  148.9 27.2 %all-to-all-done.3 = bf16[4,2,256,1024]{3,1,2,0:T(2,128)(2,1)} async-done(((bf16[4,2,256,1024]{3,1,2,0:T(2,128)(2,1)}), bf16[4,2,256,1024]{3,1,2,0:T(2,128)(2,1)}, u32[]{:S(2)}, u32[]{:S(2)}) %all-to-all-start.3) | async-done | bytes 4194336 | tf_op jit(solution)/shard_map/all_to_all | solution.py:190
  176.1 6.0 %fusion.154 = (bf16[2,1024,512]{2,0,1:T(2,128)(2,1)}, bf16[2,1024,512]{2,0,1:T(2,128)(2,1)}) fusion(bf16[2,1024,1024]{2,0,1:T(2,128)(2,1)} %bitcast.20), kind=kLoop, calls=%fused_computation.189 | loop fusion | bytes 8388608 | tf_op jit(solution)/shard_map/slice | solution.py:61
  182.1 4.7 %copy.81 = bf16[2,1024,512]{1,2,0:T(8,128)(2,1)S(1)} copy(bf16[2,1024,512]{2,0,1:T(2,128)(2,1)} %get-tuple-element.10) | data formatting | bytes 4194304
  186.9 2.5 %copy.65 = bf16[2,1024,4,128]{3,1,0,2:T(8,128)(2,1)} copy(bf16[2,1024,4,128]{1,3,2,0:T(8,128)(2,1)S(1)} %bitcast.193) | data formatting | bytes 4194304 | tf_op jit(solution)/shard_map/reshape | solution.py:60
  189.4 3.8 %fusion.155 = (f32[2,3,96]{2,1,0:T(4,128)S(1)}, f32[2,3,96,1120]{3,2,1,0:T(8,128)}) fusion(pred[2,96,1120]{2,1,0:T(8,128)(4,1)S(1)} %copy-done.10, bf16[2,1024,4,128]{3,1,0,2:T(8,128)(2,1)} %copy.65, bf16[2,96,12,128]{3,1,2,0:T(8,128)(2,1)S(1)} %fusion.32, bf16[2,96,4,128]{3,1,2,0:T(8,128)(2,1)S(1)} %copy-done.11), kind=kOutput, calls=%fused_computation.190 | convolution fusion | flops 168879200 | bytes 5245184 | tf_op jit(solution)/shard_map/sub | solution.py:81
  193.3 2.6 %fusion.160 = (f32[2,3,96]{2,1,0:T(4,128)S(1)}, f32[2,3,96,1120]{3,2,1,0:T(8,128)}) fusion(pred[2,96,1120]{2,1,0:T(8,128)(4,1)S(1)} %copy-done.10, bf16[2,1024,4,128]{3,1,0,2:T(8,128)(2,1)S(1)} %copy-done.5, bf16[2,96,12,128]{3,1,2,0:T(8,128)(2,1)S(1)} %fusion.32, bf16[2,96,4,128]{3,1,2,0:T(8,128)(2,1)S(1)} %copy-done.11), kind=kOutput, calls=%fused_computation.191 | convolution fusion | flops 168879200 | bytes 5245184 | tf_op jit(solution)/shard_map/sub | solution.py:81
  195.9 2.6 %fusion.165 = (f32[2,3,96]{2,1,0:T(4,128)S(1)}, f32[2,3,96,1120]{3,2,1,0:T(8,128)}) fusion(pred[2,96,1120]{2,1,0:T(8,128)(4,1)S(1)} %copy-done.10, bf16[2,1024,4,128]{3,1,0,2:T(8,128)(2,1)S(1)} %copy-done.5, bf16[2,96,12,128]{3,1,2,0:T(8,128)(2,1)S(1)} %fusion.32, bf16[2,96,4,128]{3,1,2,0:T(8,128)(2,1)S(1)} %copy-done.11), kind=kOutput, calls=%fused_computation.192 | convolution fusion | flops 168879200 | bytes 5245184 | tf_op jit(solution)/shard_map/sub | solution.py:81
  198.5 2.7 %fusion.170 = (f32[2,3,96]{2,1,0:T(4,128)S(1)}, f32[2,3,96,1120]{3,2,1,0:T(8,128)}) fusion(pred[2,96,1120]{2,1,0:T(8,128)(4,1)S(1)} %copy-done.10, bf16[2,1024,4,128]{3,1,0,2:T(8,128)(2,1)S(1)} %copy-done.5, bf16[2,96,12,128]{3,1,2,0:T(8,128)(2,1)S(1)} %fusion.32, bf16[2,96,4,128]{3,1,2,0:T(8,128)(2,1)S(1)} %copy-done.11), kind=kOutput, calls=%fused_computation.193 | convolution fusion | flops 168879200 | bytes 5245184 | tf_op jit(solution)/shard_map/sub | solution.py:81
  201.2 4.7 %copy.80 = bf16[2,1024,512]{1,2,0:T(8,128)(2,1)S(1)} copy(bf16[2,1024,512]{2,0,1:T(2,128)(2,1)} %get-tuple-element.9) | data formatting | bytes 4194304
  205.9 2.7 %copy.61 = bf16[2,1024,4,128]{3,1,0,2:T(8,128)(2,1)} copy(bf16[2,1024,4,128]{1,3,2,0:T(8,128)(2,1)S(1)} %bitcast.194) | data formatting | bytes 4194304 | tf_op jit(solution)/shard_map/reshape | solution.py:61
  208.6 2.6 %fusion.40 = bf16[2,96,3,128]{3,1,2,0:T(8,128)(2,1)S(1)} fusion(f32[2,3,96,1120]{3,2,1,0:T(8,128)} %get-tuple-element.22, f32[2,3,96]{2,1,0:T(4,128)S(1)} %get-tuple-element.21, bf16[2,1024,4,128]{3,1,0,2:T(8,128)(2,1)} %copy.61, bf16[2,96,4,128]{3,1,2,0:T(8,128)(2,1)S(1)} %copy-done.18), kind=kOutput, calls=%fused_computation.65 | convolution fusion | flops 167661568 | bytes 5024000 | tf_op jit(solution)/shard_map/chqk,ckd->cqhd/dot_general | solution.py:84
  (106 shorter events, 28.5 us)
Async XLA Ops:
  7.4 1.9 copy-start
  7.4 6.0 %copy-start.12 = (s32[256,1]{0,1:T(1,128)S(1)}, s32[256,1]{0,1:T(1,128)}, u32[]{:S(2)}) copy-start(s32[256,1]{0,1:T(1,128)} %param.12) | copy-start | bytes 3076
  7.4 27.1 %reduce-scatter.2.cloned.1.call-start = ((), (), s32[]{:S(2)}) async-start(), calls=%async_computation.5 | async-start | bytes 1376256 | tf_op jit(solution)/shard_map/reduce_scatter | solution.py:143
  12.8 93.7 %all-gather.2.cloned.1.call-start = ((), (), s32[]{:S(2)}) async-start(), calls=%async_computation.6 | async-start | bytes 5242880 | tf_op jit(solution)/shard_map/all_gather | solution.py:186
  14.4 15.3 %all-to-all-start = ((s32[8,1,4]{2,1,0:T(1,128)}), s32[8,1,4]{2,1,0:T(1,128)S(1)}, u32[]{:S(2)}, u32[]{:S(2)}) async-start(s32[8,1,4]{2,1,0:T(1,128)} %bitcast.1), calls=%async_computation | async-start | bytes 8192 | tf_op jit(solution)/shard_map/all_to_all | solution.py:158
  20.7 5.0 %copy-start.13 = (bf16[896]{0:T(1024)(128)(2,1)S(1)}, bf16[896]{0:T(1024)(128)(2,1)}, u32[]{:S(2)}) copy-start(bf16[896]{0:T(1024)(128)(2,1)} %param.17) | copy-start | bytes 5380
  20.7 5.0 %copy-start.6 = (bf16[896,512]{1,0:T(8,128)(2,1)S(1)}, bf16[896,512]{1,0:T(8,128)(2,1)}, u32[]{:S(2)}) copy-start(bf16[896,512]{1,0:T(8,128)(2,1)} %param.19) | copy-start | bytes 2752516
  20.7 6.3 %copy-start.15 = (s32[32]{0:T(128)S(1)}, s32[32]{0:T(128)}, u32[]{:S(2)}) copy-start(s32[32]{0:T(128)} %param.13) | copy-start | bytes 388
  20.7 6.4 %copy-start.16 = (s32[8]{0:T(128)S(1)}, s32[8]{0:T(128)}, u32[]{:S(2)}) copy-start(s32[8]{0:T(128)} %param.14) | copy-start | bytes 100
  25.6 2.7 %copy-start.7 = (bf16[896,512]{1,0:T(8,128)(2,1)S(1)}, bf16[896,512]{1,0:T(8,128)(2,1)}, u32[]{:S(2)}) copy-start(bf16[896,512]{1,0:T(8,128)(2,1)} %param.20) | copy-start | bytes 2752516
  38.0 30.1 %all-to-all-start.1 = ((bf16[8,48,448]{2,1,0:T(8,128)(2,1)}), bf16[8,48,448]{2,1,0:T(8,128)(2,1)S(1)}, u32[]{:S(2)}, u32[]{:S(2)}) async-start(bf16[8,48,448]{2,1,0:T(8,128)(2,1)} %bitcast.8), calls=%async_computation.2 | async-start | bytes 786432 | tf_op jit(solution)/shard_map/all_to_all | solution.py:151
  69.1 53.9 %all-to-all-start.2 = ((bf16[8,4,12,448]{3,0,2,1:T(8,128)(2,1)}), bf16[8,4,12,448]{3,0,2,1:T(8,128)(2,1)}, u32[]{:S(2)}, u32[]{:S(2)}) async-start(bf16[8,4,12,448]{3,0,2,1:T(8,128)(2,1)} %bitcast.9), calls=%async_computation.3 | async-start | bytes 786432 | tf_op jit(solution)/shard_map/all_to_all | solution.py:160
  123.0 53.1 %all-to-all-start.3 = ((bf16[4,2,256,1024]{3,1,2,0:T(2,128)(2,1)}), bf16[4,2,256,1024]{3,1,2,0:T(2,128)(2,1)}, u32[]{:S(2)}, u32[]{:S(2)}) async-start(bf16[4,2,256,1024]{3,1,2,0:T(2,128)(2,1)} %pad_maximum_fusion), calls=%async_computation.4 | async-start | bytes 8388608 | tf_op jit(solution)/shard_map/all_to_all | solution.py:190
  130.9 13.3 %copy-start.3 = (bf16[512,896]{1,0:T(8,128)(2,1)S(1)}, bf16[512,896]{1,0:T(8,128)(2,1)}, u32[]{:S(2)}) copy-start(bf16[512,896]{1,0:T(8,128)(2,1)} %copy.79) | copy-start | bytes 2752516
  144.6 2.2 copy-start.2
  186.9 2.6 %copy-start.10 = (pred[2,96,1120]{2,1,0:T(8,128)(4,1)S(1)}, pred[2,96,1120]{2,1,0:T(8,128)(4,1)}, u32[]{:S(2)}) copy-start(pred[2,96,1120]{2,1,0:T(8,128)(4,1)} %and_or_fusion) | copy-start | bytes 645124
  186.9 2.6 %copy-start.11 = (bf16[2,96,4,128]{3,1,2,0:T(8,128)(2,1)S(1)}, bf16[2,96,4,128]{3,1,2,0:T(8,128)(2,1)}, u32[]{:S(2)}) copy-start(bf16[2,96,4,128]{3,1,2,0:T(8,128)(2,1)} %fusion.68) | copy-start | bytes 589828
  189.4 3.8 %copy-start.5 = (bf16[2,1024,4,128]{3,1,0,2:T(8,128)(2,1)S(1)}, bf16[2,1024,4,128]{3,1,0,2:T(8,128)(2,1)}, u32[]{:S(2)}) copy-start(bf16[2,1024,4,128]{3,1,0,2:T(8,128)(2,1)} %copy.65) | copy-start | bytes 6291460
  205.9 2.7 %copy-start.18 = (bf16[2,96,4,128]{3,1,2,0:T(8,128)(2,1)S(1)}, bf16[2,96,4,128]{3,1,2,0:T(8,128)(2,1)}, u32[]{:S(2)}) copy-start(bf16[2,96,4,128]{3,1,2,0:T(8,128)(2,1)} %convolution_convert_fusion) | copy-start | bytes 589828
  208.6 2.6 %copy-start.4 = (bf16[2,1024,4,128]{3,1,0,2:T(8,128)(2,1)S(1)}, bf16[2,1024,4,128]{3,1,0,2:T(8,128)(2,1)}, u32[]{:S(2)}) copy-start(bf16[2,1024,4,128]{3,1,0,2:T(8,128)(2,1)} %copy.61) | copy-start | bytes 6291460
  208.6 3.3 %copy-start.21 = (f32[2,3,96,1120]{3,2,1,0:T(8,128)S(1)}, f32[2,3,96,1120]{3,2,1,0:T(8,128)}, u32[]{:S(2)}) copy-start(f32[2,3,96,1120]{3,2,1,0:T(8,128)} %get-tuple-element.24) | copy-start | bytes 7741444
  211.9 1.7 copy-start.20
  215.4 1.8 copy-start.14
  216.3 2.4 %copy-start.1 = (bf16[1792,896]{1,0:T(8,128)(2,1)S(1)}, bf16[1792,896]{1,0:T(8,128)(2,1)}, u32[]{:S(2)}) copy-start(bf16[1792,896]{1,0:T(8,128)(2,1)} %param.16) | copy-start | bytes 9633796
  (4 other events, 5.4 us)
Sparse Core Ops, SparseCore 0:
  12.9 21.5 reduce-scatter.1
Sparse Core Ops, SparseCore 1:
  14.8 91.6 all-gather.1
